TPU v7x, 32 devices: a whole 2x2x4 slice. The times are simulated.
32 devices in a mesh: blk: 8 (over z, y), rep: 4 (over x, core).
Axes of the slice: x: 2, y: 2, z: 4, core: 2. Of those that a mesh axis runs over, the one named last changes fastest.
Arguments:
- embeddings: bfloat16 [1024, 256], P('blk'), may hold values from -21 to 21
- targets: float32 [128, 1024], P('rep', 'blk'), may hold values from -180 to 180
Outputs:
- solution: float32 [128, 1024], P('rep', 'blk')
- residual: float32 [128, 1024], P('rep', 'blk')
All inputs are finite; a program needn't handle non-finite values.
Results may differ from a plain program's by a relative error of at most 0.0003.
Values may be sent and summed in bfloat16 or wider, within the bound.
A program may use at most 64 MiB of HBM per device.

v0:
```python
import jax
import jax.numpy as jnp
from jax import lax
from jax.sharding import PartitionSpec as P

ITERS = 2
length_scale = 1.0
noise_var = 1.0


def squared_norms(points):
    widened = points.astype(jnp.float32)
    return jnp.sum(widened * widened, axis=1)


def kernel_tile(own_points, own_norms, own_labels, far_points, far_norms, far_labels):
    products = jnp.einsum("pd,qd->pq", own_points, far_points, preferred_element_type=jnp.float32)
    distance_sq = own_norms[:, None] + far_norms[None, :] - 2.0 * products
    distance_sq = jnp.where(own_labels[:, None] == far_labels[None, :], 0.0, distance_sq)
    return jnp.exp(-jnp.sqrt(distance_sq) / length_scale)


def paired(residual, image):
    return lax.psum((jnp.sum(residual * residual), jnp.sum(residual * image)), ("blk", "rep"))


def per_device(embeddings, targets):
    block_id = lax.axis_index("blk")
    local_count = embeddings.shape[0]
    own_norms = squared_norms(embeddings)
    own_labels = block_id * local_count + jnp.arange(local_count, dtype=jnp.int32)
    everyone = lax.all_gather(embeddings, "blk", axis=0, tiled=True)
    every_norms = squared_norms(everyone)

    def folded_image(direction):
        piece = lax.all_gather(direction, "blk", axis=1, tiled=True)
        count = piece.shape[1]
        far_labels = jnp.arange(count, dtype=jnp.int32)
        tile = kernel_tile(embeddings, own_norms, own_labels, everyone, every_norms, far_labels)
        total = jnp.einsum(
            "rq,pq->rp",
            piece,
            tile,
            precision=lax.Precision.HIGHEST,
            preferred_element_type=jnp.float32,
        )
        return total + noise_var * direction

    solution = jnp.zeros_like(targets)
    residual = targets
    image = folded_image(residual)
    norm_now, product = paired(residual, image)
    alpha = norm_now / product
    direction = residual
    along = image
    for iteration in range(ITERS):
        solution = solution + alpha * direction
        residual = residual - alpha * along
        if iteration + 1 < ITERS:
            image = folded_image(residual)
            norm_next, product = paired(residual, image)
            ratio = norm_next / norm_now
            alpha = norm_next / (product - ratio * norm_next / alpha)
            direction = residual + ratio * direction
            along = image + ratio * along
            norm_now = norm_next
    return (solution, residual)


def solution(mesh):
    in_specs = (P("blk", None), P("rep", "blk"))
    out_specs = (P("rep", "blk"), P("rep", "blk"))
    return jax.shard_map(
        per_device, mesh=mesh, in_specs=in_specs, out_specs=out_specs, check_vma=False
    )
```

profile of v0, /device:TPU:14, one launch (start us, length us, event | category | flops | bytes accessed | tf_op | source)
XLA Modules:
  0.0 184.3 jit_solution(12723505699822419723)
XLA Ops:
  0.6 29.7 %all_gather.9 = bf16[1024,256]{1,0:T(8,128)(2,1)S(1)} all-gather(bf16[128,256]{1,0:T(8,128)(2,1)} %param.2), channel_id=1, replica_groups=mesh['blk'=8,'rep'=4] {'blk'}, dimensions={0}, use_global_device_ids=true | all-gather | bytes 589824 | tf_op jit(solution)/shard_map/all_gather | solution.py:32
  30.3 0.0 copy-start.1
  30.3 0.2 multiply_reduce_fusion
  30.5 0.6 copy-done.1
  31.1 0.1 multiply_reduce_fusion.1
  31.2 0.0 copy-start
  31.2 0.5 fusion.4
  31.7 0.3 copy-done
  32.0 30.0 %all_gather.10 = f32[32,1024]{1,0:T(8,128)S(1)} all-gather(f32[32,128]{1,0:T(8,128)S(1)} %copy-done), channel_id=1, replica_groups=mesh['blk'=8,'rep'=4] {'blk'}, dimensions={1}, use_global_device_ids=true | all-gather | bytes 147456 | tf_op jit(solution)/shard_map/all_gather | solution.py:36
  62.0 1.2 multiply_reduce_fusion.4
  63.2 43.1 %all-reduce.1 = (f32[]{:T(128)}, f32[]{:T(128)}) all-reduce(f32[]{:T(128)} %get-tuple-element.5, f32[]{:T(128)} %get-tuple-element.4), channel_id=1, replica_groups=mesh['blk'=8,'rep'=4] {'blk','rep'}, use_global_device_ids=true, to_apply=%region_1.0 | all-reduce | flops 2 | bytes 16 | tf_op jit(solution)/shard_map/psum | solution.py:24
  107.7 25.4 %all_gather.11 = f32[32,1024]{1,0:T(8,128)S(1)} all-gather(f32[32,128]{1,0:T(8,128)S(1)} %multiply_subtract_fusion.1), channel_id=1, replica_groups=mesh['blk'=8,'rep'=4] {'blk'}, dimensions={1}, use_global_device_ids=true | all-gather | bytes 147456 | tf_op jit(solution)/shard_map/all_gather | solution.py:36
  133.1 1.3 multiply_reduce_fusion.2
  134.4 44.7 %all-reduce = (f32[]{:T(128)}, f32[]{:T(128)}) all-reduce(f32[]{:T(128)} %get-tuple-element.3, f32[]{:T(128)} %get-tuple-element.2), channel_id=1, replica_groups=mesh['blk'=8,'rep'=4] {'blk','rep'}, use_global_device_ids=true, to_apply=%region_7.8 | all-reduce | flops 2 | bytes 16 | tf_op jit(solution)/shard_map/psum | solution.py:24
  183.7 0.6 multiply_subtract_fusion
  (2 shorter events, 0.0 us)
Async XLA Ops:
  30.3 0.8 copy-start.1
  31.2 0.7 copy-start
where the time goes:
time: 185 us; the launch traced here: 184 us
  blocking collectives  173 us (94%)
  between operations  6.58 us (4%)
  matrix products  2.96 us (2%)
    psum x2, blocking collectives, paired(): lax.psum((jnp.sum(residual * residual), jnp.sum(residual * image)), ('blk...  87.8 us
    all_gather x2, blocking collectives, folded_image(): piece = lax.all_gather(direction, 'blk', axis=1, tiled=True)  55.5 us
    all_gather x1, blocking collectives, per_device(): everyone = lax.all_gather(embeddings, 'blk', axis=0, tiled=True)  29.7 us

commit v1 on v0

--- a/solution.py
+++ b/solution.py
@@ -21,7 +21,9 @@
 
 
 def paired(residual, image):
-    return lax.psum((jnp.sum(residual * residual), jnp.sum(residual * image)), ("blk", "rep"))
+    return lax.psum(
+        lax.psum((jnp.sum(residual * residual), jnp.sum(residual * image)), "rep"), "blk"
+    )
 
 
 def per_device(embeddings, targets):

time: 185 us -> 159 us (0.86)
  the two profiles are of different devices: /device:TPU:14 before, /device:TPU:0 now
where the time goes in v1:
time: 159 us; the launch traced here: 158 us
  blocking collectives  147 us (92%)
  between operations  6.58 us (4%)
  matrix products  2.94 us (2%)
    all_gather x2, blocking collectives, folded_image(): piece = lax.all_gather(direction, 'blk', axis=1, tiled=True)  61 us
    psum x2, blocking collectives, paired(): lax.psum(lax.psum((jnp.sum(residual * residual), jnp.sum(residual * image...  40 us
    all_gather x1, blocking collectives, per_device(): everyone = lax.all_gather(embeddings, 'blk', axis=0, tiled=True)  33.2 us
    psum x2, blocking collectives, paired(): lax.psum((jnp.sum(residual * residual), jnp.sum(residual * image)), 'rep')  12.6 us

profile of v1, /device:TPU:0, one launch (start us, length us, event | category | flops | bytes accessed | tf_op | source)
XLA Modules:
  0.0 158.2 jit_solution(855782369501122017)
XLA Ops:
  0.6 33.2 %all_gather.9 = bf16[1024,256]{1,0:T(8,128)(2,1)S(1)} all-gather(bf16[128,256]{1,0:T(8,128)(2,1)} %param.2), channel_id=1, replica_groups=mesh['blk'=8,'rep'=4] {'blk'}, dimensions={0}, use_global_device_ids=true | all-gather | bytes 589824 | tf_op jit(solution)/shard_map/all_gather | solution.py:34
  33.9 0.0 copy-start.1
  33.9 0.2 multiply_reduce_fusion
  34.1 0.6 copy-done.1
  34.7 0.1 multiply_reduce_fusion.1
  34.8 0.0 copy-start
  34.8 0.5 fusion.4
  35.3 0.3 copy-done
  35.6 30.5 %all_gather.10 = f32[32,1024]{1,0:T(8,128)S(1)} all-gather(f32[32,128]{1,0:T(8,128)S(1)} %copy-done), channel_id=1, replica_groups=mesh['blk'=8,'rep'=4] {'blk'}, dimensions={1}, use_global_device_ids=true | all-gather | bytes 147456 | tf_op jit(solution)/shard_map/all_gather | solution.py:38
  66.1 1.2 multiply_reduce_fusion.4
  67.3 6.3 %all-reduce.3 = (f32[]{:T(128)}, f32[]{:T(128)}) all-reduce(f32[]{:T(128)} %get-tuple-element.5, f32[]{:T(128)} %get-tuple-element.4), channel_id=1, replica_groups=mesh['blk'=8,'rep'=4] {'rep'}, use_global_device_ids=true, to_apply=%region_1.0 | all-reduce | flops 2 | bytes 16 | tf_op jit(solution)/shard_map/psum | solution.py:25
  73.5 22.2 %all-reduce.1 = (f32[]{:T(128)}, f32[]{:T(128)}) all-reduce(f32[]{:T(128)} %get-tuple-element.12, f32[]{:T(128)} %get-tuple-element.13), channel_id=1, replica_groups=mesh['blk'=8,'rep'=4] {'blk'}, use_global_device_ids=true, to_apply=%region_2.3 | all-reduce | flops 2 | bytes 16 | tf_op jit(solution)/shard_map/psum | solution.py:24
  97.0 30.5 %all_gather.11 = f32[32,1024]{1,0:T(8,128)S(1)} all-gather(f32[32,128]{1,0:T(8,128)S(1)} %multiply_subtract_fusion.1), channel_id=1, replica_groups=mesh['blk'=8,'rep'=4] {'blk'}, dimensions={1}, use_global_device_ids=true | all-gather | bytes 147456 | tf_op jit(solution)/shard_map/all_gather | solution.py:38
  127.6 1.3 multiply_reduce_fusion.2
  128.9 6.3 %all-reduce.2 = (f32[]{:T(128)}, f32[]{:T(128)}) all-reduce(f32[]{:T(128)} %get-tuple-element.3, f32[]{:T(128)} %get-tuple-element.2), channel_id=1, replica_groups=mesh['blk'=8,'rep'=4] {'rep'}, use_global_device_ids=true, to_apply=%region_9.10 | all-reduce | flops 2 | bytes 16 | tf_op jit(solution)/shard_map/psum | solution.py:25
  135.2 17.8 %all-reduce = (f32[]{:T(128)}, f32[]{:T(128)}) all-reduce(f32[]{:T(128)} %get-tuple-element.10, f32[]{:T(128)} %get-tuple-element.11), channel_id=1, replica_groups=mesh['blk'=8,'rep'=4] {'blk'}, use_global_device_ids=true, to_apply=%region_10.11 | all-reduce | flops 2 | bytes 16 | tf_op jit(solution)/shard_map/psum | solution.py:24
  157.6 0.6 multiply_subtract_fusion
  (2 shorter events, 0.0 us)
Async XLA Ops:
  33.9 0.8 copy-start.1
  34.8 0.7 copy-start
